TPU v7x, 256 devices: a whole 4x4x8 slice. The times are simulated.
256 devices in a mesh: coord: 64 (over y, x_lo, z), ka: 4 (over x_hi, core).
Axes of the slice: x: 4 (x_hi: 2, x_lo: 2; x = x_hi * 2 + x_lo), y: 4, z: 8, core: 2. Of those that a mesh axis runs over, the one named last changes fastest.
Arguments:
- states: float32 [4, 512, 512, 128], P('ka', 'coord'), may hold values from -6 to 6
- potential: float32 [512, 512, 128], P('coord'), may hold values from 0 to 3
- rotation_factor: float32 [512, 512], P('coord'), may hold values from 0.05 to 0.4
- basis_first: float32 [512, 512], replicated, may hold values from -0.25 to 0.25
- basis_second: float32 [512, 512], replicated, may hold values from -0.25 to 0.25
- basis_third: float32 [128, 128], replicated, may hold values from -0.5 to 0.5
- levels_first: float32 [512], replicated, may hold values from 0 to 2
- levels_second: float32 [512], replicated, may hold values from 0 to 2
- levels_third: float32 [128], replicated, may hold values from 0 to 2
- kinetic_first: float32 [512, 512], replicated, as said below
- kinetic_second: float32 [512, 512], replicated, as said below
- kinetic_third: float32 [128, 128], replicated, as said below
- coriolis_matrix: float32 [128, 128], replicated, may hold values from -0.5 to 0.5
Outputs:
- correction: float32 [4, 512, 512, 128], P('ka', 'coord')
- residual: float32 [4, 512, 512, 128], P('ka', 'coord')
Inputs may be any that keep to these rules, and one draw needn't show every extreme that they name: `kinetic_first`: symmetric. `kinetic_second`: symmetric. `kinetic_third`: symmetric.
All inputs are finite; a program needn't handle non-finite values.
Results may differ from a plain program's by a relative error of at most 0.000052.
Values sent between devices are 32-bit elements; how exact they have to be, the bound alone decides.
A program may use at most 128 MiB of HBM per device.

v0:
```python
import functools
import math

import jax
import jax.numpy as jnp
from jax import lax
from jax.experimental import pallas as pl
from jax.experimental.pallas import tpu as pltpu
from jax.sharding import PartitionSpec as P

MESH = pl.DeviceIdType.MESH
f32 = jnp.float32
bf16 = jnp.bfloat16
shift_energy = 2.5
damping = 0.5

PEERS = 64
BLOCKS = 4
GROUPS = 4
N1 = 512
N2 = 512
N3 = 128
ROWS = N1 // PEERS
PAIRS = ROWS // 2
SPAN = N2 // GROUPS
OWN = 4
HALVES = OWN // 2
PLANES = 8
NEAR = 4
LINES = PEERS // PLANES
SERVED = NEAR * LINES


def split(value):
    high = value.astype(bf16)
    return high, (value - high.astype(f32)).astype(bf16)


def dot(left, right):
    return jnp.dot(left, right, preferred_element_type=f32)


def put_weight(ref, value, offset=0, base=0):
    high, low = split(value)
    width = value.shape[1]
    for place, part in enumerate((high, low, high)):
        lanes = pl.ds(pl.multiple_of(base + place * width, N3), width)
        ref[pl.ds(offset, value.shape[0]), lanes] = part


def put_data(ref, value, lane, base=0):
    high, low = split(value)
    height, width = value.shape
    for place, part in enumerate((high, high, low)):
        rows = pl.ds(pl.multiple_of(base + place * height, N3), height)
        ref[rows, pl.ds(lane, width)] = part


def spread(row, height=N3):
    return jnp.broadcast_to(row, (height, row.shape[1])).T


def kernel(
    states,
    potential,
    rotation,
    first,
    second,
    third,
    levels_first,
    levels_second,
    levels_third,
    kin_first,
    kin_second,
    kin_third,
    coriolis,
    solved_out,
    residual_out,
    src,
    pot,
    rot,
    b1,
    b2,
    k1,
    k2,
    b3,
    k3,
    cor,
    w_b2t,
    w_b1t,
    w_tmp,
    w_xy,
    w_b2,
    w_kb,
    u1,
    u2,
    cols,
    xs,
    ys,
    xr,
    yr,
    above,
    below,
    data,
    lx,
    ly,
    t1,
    t2,
    tv,
    angular,
    w_c,
    w_a,
    w_al,
    w_b,
    w_v,
    w_vl,
    acc_v,
    diag,
    wide,
    lev1,
    picked,
    load_sem,
    out_sem,
    fwd_send,
    fwd_recv,
    hand_send,
    hand_recv,
    x_send,
    x_recv,
    y_send,
    y_recv,
    up_send,
    up_recv,
    down_send,
    down_recv,
):
    me = lax.axis_index("coord")
    ka = lax.axis_index("ka")
    my_y, my_x, my_z = me // 16, lax.rem(me // 8, 2), lax.rem(me, 8)
    my_line = me // PLANES

    def side(g):
        return lax.rem(my_z + lax.rem(g, 2), 2)

    def pair_of(g):
        return lax.rem(my_z - lax.rem(g, 2) + PLANES, PLANES) // 2

    def near_plane(g, n):
        return lax.rem(my_z + (2 * side(g) - 1) * n + PLANES, PLANES)

    def line(step):
        return lax.rem(my_y + step // 2, 4) * 2 + lax.rem(my_x + step, 2)

    def loop(start, stop, body):
        def step(s, carry):
            body(s)
            return carry

        lax.fori_loop(start, stop, step, 0)

    loads = [
        pltpu.make_async_copy(source, target, load_sem.at[index])
        for index, (source, target) in enumerate(
            (
                (second, b2),
                (states.at[0], src),
                (third, b3),
                (first, b1),
                (kin_first, k1),
                (kin_third, k3),
                (coriolis, cor),
                (kin_second, k2),
                (potential, pot),
                (rotation, rot),
            )
        )
    ]
    for copy in loads[:2]:
        copy.start()
    barrier = pltpu.get_barrier_semaphore()
    def greet(s):
        p = line(s // PLANES) * PLANES + lax.rem(my_z + s, PLANES)
        pl.semaphore_signal(barrier, inc=1, device_id=(p, ka), device_id_type=MESH)

    loop(1, PEERS, greet)

    @pl.when(ka > 0)
    def _():
        pl.semaphore_signal(barrier, inc=1, device_id=(me, ka - 1), device_id_type=MESH)

    @pl.when(ka < BLOCKS - 1)
    def _():
        pl.semaphore_signal(barrier, inc=1, device_id=(me, ka + 1), device_id_type=MESH)

    loads[0].wait()

    loads[1].wait()
    for copy in loads[2:]:
        copy.start()

    @pl.loop(0, PAIRS)
    def _(pair):
        for t in range(2):
            put_data(u1.at[pair], src[2 * pair + t], t * N3)

    def way_out(g):
        rows = pl.ds(pl.multiple_of(g * SPAN, SPAN), SPAN)
        put_weight(w_b2t, b2[:, rows].T)
        for pair in range(PAIRS):
            out = dot(w_b2t[...], u1[pair])
            u2[rows, 2 * pair, :] = out[:, 0:N3]
            u2[rows, 2 * pair + 1, :] = out[:, N3:]

        @pl.when(g == 0)
        def _():
            @pl.when(jnp.logical_or(ka == 0, ka == BLOCKS - 1))
            def _():
                pl.semaphore_wait(barrier, PEERS)

            @pl.when(jnp.logical_and(ka > 0, ka < BLOCKS - 1))
            def _():
                pl.semaphore_wait(barrier, PEERS + 1)

        turn = lax.rem(g, 2)

        def place(s):
            where = line(s // 4)
            pair = lax.rem(pair_of(g) + s, 4)
            away = lax.rem(my_z - turn - 2 * pair + 2 * PLANES, PLANES)
            upper = jnp.logical_and(away >= 1, away <= NEAR).astype(jnp.int32)
            plane = lax.rem(2 * pair + upper + turn, PLANES)
            return g * SPAN + (where * 4 + pair) * OWN, where * PLANES + plane

        def send(s):
            column, p = place(s)
            pltpu.make_async_remote_copy(
                u2.at[pl.ds(column, OWN)],
                cols.at[g, :, my_line, my_z],
                fwd_send.at[g],
                fwd_recv.at[g],
                device_id=(p, ka),
                device_id_type=MESH,
            ).start()

        loop(1, SERVED, send)
        pltpu.make_async_copy(
            u2.at[pl.ds(place(0)[0], OWN)], cols.at[g, :, my_line, my_z], fwd_recv.at[g]
        ).start()

    def hand_over(g):
        pltpu.make_async_copy(cols.at[g, 0:HALVES], cols.at[g, 0:HALVES], fwd_recv.at[g]).wait()
        partner = lax.rem(my_z + 1 - 2 * side(g) + PLANES, PLANES)
        for n in range(NEAR):
            part = cols.at[g, :, :, near_plane(g, n)]
            pltpu.make_async_remote_copy(
                part,
                part,
                hand_send.at[g],
                hand_recv.at[g],
                device_id=(my_line * PLANES + partner, ka),
                device_id_type=MESH,
            ).start()

    def give(g, buffer, target, send_sem, recv_sem):
        home = pl.ds(g * SPAN + (my_line * 4 + pair_of(g)) * OWN, OWN)

        def send(s):
            where, n = line(s // NEAR), lax.rem(s, NEAR)
            pltpu.make_async_remote_copy(
                buffer.at[g, :, n, where],
                target.at[home],
                send_sem.at[g],
                recv_sem.at[g],
                device_id=(where * PLANES + near_plane(g, n), ka),
                device_id_type=MESH,
            ).start()

        loop(1, SERVED, send)
        pltpu.make_async_copy(
            buffer.at[g, :, 0, my_line], target.at[home], recv_sem.at[g]
        ).start()

    def in_columns(g):
        pltpu.make_async_copy(cols.at[g, 0:HALVES], cols.at[g, 0:HALVES], hand_recv.at[g]).wait()

        @pl.loop(0, HALVES)
        def _(half):
            for t in range(2):
                high, low = split(cols[g, 2 * half + t].reshape(N1, N3))
                lx[0:N1, 0:N3] = high
                lx[0:N1, N3:] = low
                both = dot(lx[0:N1, :], w_c[...])
                put_data(data, both[:, 0:N3] + both[:, N3:], t * N3)
            coeff = dot(w_b1t[...], data[...])
            for t in range(2):
                column = g * SPAN + (my_line * 4 + pair_of(g)) * OWN + 2 * half + t
                level = (
                    lev1[...] + levels_second[column] + levels_third[...] - shift_energy
                )
                filt = level / (level * level + damping * damping)
                put_data(data, coeff[:, t * N3 : (t + 1) * N3] * filt, t * N3)
            out = dot(w_xy[lax.rem(g, 2)], data[...])
            for t in range(2):
                part = out[:, t * N3 : (t + 1) * N3].reshape(2, NEAR, LINES, ROWS, N3)
                xs[g, 2 * half + t] = part[0]
                ys[g, 2 * half + t] = part[1]

        give(g, xs, xr, x_send, x_recv)

    def give_bent(g):
        give(g, ys, yr, y_send, y_recv)

    def in_slab(g):
        rows = pl.ds(pl.multiple_of(g * SPAN, SPAN), SPAN)
        pltpu.make_async_copy(xr.at[rows], xr.at[rows], x_recv.at[g]).wait()

        @pl.when(ka > 0)
        def _():
            pltpu.make_async_remote_copy(
                xr.at[rows],
                above.at[rows],
                up_send.at[g],
                up_recv.at[g],
                device_id=(me, ka - 1),
                device_id_type=MESH,
            ).start()

        @pl.when(ka < BLOCKS - 1)
        def _():
            pltpu.make_async_remote_copy(
                xr.at[rows],
                below.at[rows],
                down_send.at[g],
                down_recv.at[g],
                device_id=(me, ka + 1),
                device_id_type=MESH,
            ).start()

        @pl.when(g > 0)
        def _():
            give_bent(g - 1)

        @pl.when(g == GROUPS - 1)
        def _():
            give_bent(g)

        for i in range(ROWS):
            high, low = split(xr[rows, i, :])
            lx[i * SPAN : (i + 1) * SPAN, 0:N3] = high
            lx[i * SPAN : (i + 1) * SPAN, N3:] = low

        @pl.loop(0, PAIRS)
        def _(pair):
            for t in range(2):
                at = pl.ds(pl.multiple_of((2 * pair + t) * SPAN, SPAN), SPAN)
                here = dot(lx[at, :], w_a[...]) + dot(lx[at, 0:N3], w_al[...])
                put_data(t1.at[pair], here[:, 0:N3], t * N3, lax.rem(g, 2) * 3 * SPAN)
                angular[2 * pair + t, rows, :] = here[:, N3:]

        @pl.when(lax.rem(g, 2) == 1)
        def _():
            both = pl.ds(pl.multiple_of(g // 2 * 6 * SPAN, 6 * SPAN), 6 * SPAN)

            @pl.loop(0, PAIRS)
            def _(pair):
                out = dot(w_b2[:, both], t1[pair])
                for t in range(2):
                    pot[2 * pair + t] += out[:, t * N3 : (t + 1) * N3]
                out = dot(w_kb[:, both], t1[pair])
                for t in range(2):
                    src[2 * pair + t] -= out[:, t * N3 : (t + 1) * N3]

    def between_blocks(g, last=False):
        rows = pl.ds(pl.multiple_of(g * SPAN, SPAN), SPAN)

        @pl.when(ka < BLOCKS - 1)
        def _():
            pltpu.make_async_copy(above.at[rows], above.at[rows], up_recv.at[g]).wait()

        @pl.when(ka > 0)
        def _():
            pltpu.make_async_copy(below.at[rows], below.at[rows], down_recv.at[g]).wait()

        for i in range(ROWS):
            at = slice(i * SPAN, (i + 1) * SPAN)
            high, low = split(above[rows, i, :])
            lx[at, 0:N3] = high
            ly[at, 0:N3] = low
            high, low = split(below[rows, i, :])
            lx[at, N3:] = high
            ly[at, N3:] = low

        @pl.loop(0, PAIRS)
        def _(pair):
            for t in range(2):
                at = pl.ds(pl.multiple_of((2 * pair + t) * SPAN, SPAN), SPAN)
                mixed = dot(lx[at, :], w_v[...])
                mixed = mixed[:, 0:N3] + mixed[:, N3:] + dot(ly[at, :], w_vl[...])
                put_data(tv.at[pair], mixed, t * N3, lax.rem(g, 2) * 3 * SPAN)

        @pl.when(lax.rem(g, 2) == 1)
        def _():
            both = pl.ds(pl.multiple_of(g // 2 * 6 * SPAN, 6 * SPAN), 6 * SPAN)

            @pl.loop(0, PAIRS)
            def _(pair):
                out = dot(w_b2[:, both], tv[pair])
                for t in range(2):
                    acc_v[2 * pair + t] += out[:, t * N3 : (t + 1) * N3]
                if last:
                    two = pl.ds(2 * pair, 2)
                    src[two] -= wide[two] * acc_v[two]
                    pltpu.make_async_copy(
                        src.at[two], residual_out.at[0, two], out_sem.at[1]
                    ).start()

    way_out(0)

    @pl.loop(0, 2 * GROUPS - 1)
    def _(step):
        @pl.when(step == 0)
        def _():
            way_out(1)

            loads[2].wait()
            high, low = split(b3[...])
            w_c[0:N3, 0:N3] = high
            w_c[N3:, 0:N3] = high
            w_c[0:N3, N3:] = low
            w_c[N3:, N3:] = jnp.zeros((N3, N3), bf16)
            loads[3].wait()

            @pl.loop(0, N1 // N3)
            def _(n):
                at = pl.multiple_of(n * N3, N3)
                put_weight(w_b1t, b1[:, pl.ds(at, N3)].T, at)

            for n in range(N1 // N3):
                lev1[n * N3 : (n + 1) * N3, :] = spread(levels_first[n : n + 1, :])


        @pl.when(step < GROUPS)
        def _():
            hand_over(step)

        @pl.when(step < GROUPS - 2)
        def _():
            way_out(step + 2)

        @pl.when(step == 0)
        def _():
            loads[4].wait()

            for turn in range(2):

                def gather(s, turn=turn):
                    start = pl.multiple_of(
                        lax.rem(s, LINES) * PLANES * ROWS + near_plane(turn, s // LINES) * ROWS, ROWS
                    )
                    to = pl.multiple_of(s * ROWS, ROWS)
                    picked[pl.ds(to, ROWS), :] = b1[pl.ds(start, ROWS), :]
                    picked[pl.ds(N1 // 2 + to, ROWS), :] = k1[pl.ds(start, ROWS), :]

                loop(0, SERVED, gather)

                @pl.loop(0, 2)
                def _(half, turn=turn):
                    at = pl.multiple_of(half * N3, N3)
                    put_weight(w_xy.at[turn], picked[pl.ds(at, N3), :], at)
                    put_weight(w_tmp, picked[pl.ds(N1 // 2 + at, N3), :], at)

                @pl.loop(0, 2)
                def _(half):
                    at = pl.ds(pl.multiple_of(half * 256, 256), 256)
                    put_data(data, b1[:, at], 0)
                    picked[N1 // 2 :, at] = dot(w_tmp[0 : N1 // 2, :], data[...])

                @pl.loop(0, 2)
                def _(half, turn=turn):
                    at = pl.multiple_of(N1 // 2 + half * N3, N3)
                    put_weight(w_xy.at[turn], picked[pl.ds(at, N3), :], at)


        @pl.when(step == 1)
        def _():
            loads[5].wait()
            loads[6].wait()
            kval = ka.astype(f32)
            reach = [math.sqrt((BLOCKS - 1) * BLOCKS - k * (k + 1)) for k in range(BLOCKS)]

            def by_block(values):
                out = f32(values[-1])
                for k in range(BLOCKS - 1):
                    out = jnp.where(ka == k, f32(values[k]), out)
                return out

            coupled_up = by_block(reach)
            coupled_down = by_block([0.0] + reach[:-1])
            turned = b3[...].T
            exact = functools.partial(
                jnp.dot, preferred_element_type=f32, precision=lax.Precision.HIGHEST
            )
            high, low = split(turned)
            high_k, low_k = split(exact(turned, k3[...].T))
            w_a[0:N3, 0:N3] = high
            w_a[N3:, 0:N3] = high
            w_a[0:N3, N3:] = high_k
            w_a[N3:, N3:] = high_k
            w_al[:, 0:N3] = low
            w_al[:, N3:] = low_k
            w_b[0:N3, 0:N3] = high
            w_b[N3:, 0:N3] = high
            w_b[0:N3, N3:] = low
            w_b[N3:, N3:] = jnp.zeros((N3, N3), bf16)
            high, low = split(exact(turned, cor[...].T) * coupled_up)
            w_v[0:N3, 0:N3] = high
            w_v[0:N3, N3:] = low
            w_vl[0:N3, :] = high
            high, low = split(exact(turned, cor[...]) * coupled_down)
            w_v[N3:, 0:N3] = high
            w_v[N3:, N3:] = low
            w_vl[N3:, :] = high

            @pl.loop(0, GROUPS)
            def _(g):
                part = b2[:, pl.ds(pl.multiple_of(g * SPAN, SPAN), SPAN)]
                put_weight(w_b2, part, 0, g * 3 * SPAN)

            loads[7].wait()

            @pl.loop(0, N2 // N3)
            def _(n):
                at = pl.multiple_of(n * N3, N3)
                put_weight(w_tmp, k2[pl.ds(at, N3), :], at)

            @pl.loop(0, 2)
            def _(half):
                put_data(data, b2[:, pl.ds(pl.multiple_of(half * 256, 256), 256)], 0)
                out = dot(w_tmp[...], data[...])
                for n in range(256 // SPAN):
                    part = out[:, n * SPAN : (n + 1) * SPAN]
                    put_weight(w_kb, part, 0, (half * (256 // SPAN) + n) * 3 * SPAN)

            loads[8].wait()
            loads[9].wait()

            @pl.loop(0, N2 // N3)
            def _(n):
                at = pl.ds(pl.multiple_of(n * N3, N3), N3)
                factors = rot[:, at]
                for i in range(ROWS):
                    factor = spread(factors[i : i + 1, :])
                    wide[i, at, :] = factor
                    diag[i, at, :] = pot[i, at, :] + kval * kval * factor - shift_energy
                    pot[i, at, :] = jnp.zeros((N3, N3), f32)
                    acc_v[i, at, :] = jnp.zeros((N3, N3), f32)

            @pl.when(ka == 0)
            def _():
                below[...] = jnp.zeros(below.shape, f32)

            @pl.when(ka == BLOCKS - 1)
            def _():
                above[...] = jnp.zeros(above.shape, f32)


        @pl.when(jnp.logical_and(step >= 1, step <= GROUPS))
        def _():
            in_columns(step - 1)

        @pl.when(step >= GROUPS - 1)
        def _():
            in_slab(step - GROUPS + 1)

        @pl.when(step > GROUPS)
        def _():
            between_blocks(step - GROUPS - 1)

    results = [pltpu.make_async_copy(pot, solved_out.at[0], out_sem.at[0])]
    results[0].start()
    between_blocks(GROUPS - 2)

    @pl.loop(0, ROWS)
    def _(i):
        src[i] -= diag[i] * pot[i]

    @pl.loop(0, GROUPS)
    def _(g):
        rows = pl.ds(pl.multiple_of(g * SPAN, SPAN), SPAN)
        pltpu.make_async_copy(yr.at[rows], yr.at[rows], y_recv.at[g]).wait()
        for i in range(ROWS):
            high, low = split(yr[rows, i, :])
            ly[i * SPAN : (i + 1) * SPAN, 0:N3] = high
            ly[i * SPAN : (i + 1) * SPAN, N3:] = low

        @pl.loop(0, PAIRS)
        def _(pair):
            for t in range(2):
                at = pl.ds(pl.multiple_of((2 * pair + t) * SPAN, SPAN), SPAN)
                bent = dot(ly[at, :], w_b[...])
                bent = bent[:, 0:N3] + bent[:, N3:] + angular[2 * pair + t, rows, :]
                put_data(t2.at[pair], bent, t * N3)
            each = pl.ds(pl.multiple_of(g * 3 * SPAN, 3 * SPAN), 3 * SPAN)
            out = dot(w_b2[:, each], t2[pair])
            for t in range(2):
                src[2 * pair + t] -= out[:, t * N3 : (t + 1) * N3]

    between_blocks(GROUPS - 1, last=True)
    results.append(pltpu.make_async_copy(src, residual_out.at[0], out_sem.at[1]))

    @pl.loop(0, GROUPS)
    def _(g):
        rows = pl.ds(g * SPAN, SPAN)
        part = u2.at[pl.ds(0, (SERVED - 1) * OWN)]
        pltpu.make_async_copy(part, part, fwd_send.at[g]).wait()
        pltpu.make_async_copy(part, part, x_send.at[g]).wait()
        pltpu.make_async_copy(part, part, y_send.at[g]).wait()
        pltpu.make_async_copy(cols.at[g, 0:HALVES], cols.at[g, 0:HALVES], hand_send.at[g]).wait()

        @pl.when(ka > 0)
        def _():
            pltpu.make_async_copy(xr.at[rows], xr.at[rows], up_send.at[g]).wait()

        @pl.when(ka < BLOCKS - 1)
        def _():
            pltpu.make_async_copy(xr.at[rows], xr.at[rows], down_send.at[g]).wait()

    for copy in results:
        copy.wait()


def per_device(
    states,
    potential,
    rotation_factor,
    basis_first,
    basis_second,
    basis_third,
    levels_first,
    levels_second,
    levels_third,
    kinetic_first,
    kinetic_second,
    kinetic_third,
    coriolis_matrix,
):
    vmem, dma = pltpu.VMEM, pltpu.SemaphoreType.DMA
    anywhere = pl.BlockSpec(memory_space=pl.ANY)
    here = pl.BlockSpec(memory_space=pltpu.VMEM)
    slab = (ROWS, N2, N3)
    turned = (N2, ROWS, N3)
    columns = (GROUPS, OWN, LINES, PLANES, ROWS, N3)
    given = (GROUPS, OWN, NEAR, LINES, ROWS, N3)
    weight = vmem((N1, 3 * N1), bf16)
    parts = vmem((N2, GROUPS * 3 * SPAN), bf16)
    stacked = vmem((PAIRS, 6 * SPAN, 2 * N3), bf16)
    square = vmem((N1, N1), f32)
    small = vmem((N3, N3), f32)
    scratch = [
        vmem(slab, f32),
        vmem(slab, f32),
        vmem((ROWS, N2), f32),
        square,
        square,
        square,
        square,
        small,
        small,
        small,
        vmem((SPAN, 3 * N2), bf16),
        weight,
        weight,
        vmem((2, N1, 3 * N1), bf16),
        parts,
        parts,
        vmem((PAIRS, 3 * N2, 2 * N3), bf16),
        vmem(turned, f32),
        vmem(columns, f32),
        vmem(given, f32),
        vmem(given, f32),
        vmem(turned, f32),
        vmem(turned, f32),
        vmem(turned, f32),
        vmem(turned, f32),
        vmem((3 * N1, 2 * N3), bf16),
        vmem((ROWS * SPAN, 2 * N3), bf16),
        vmem((ROWS * SPAN, 2 * N3), bf16),
        stacked,
        vmem((PAIRS, 3 * SPAN, 2 * N3), bf16),
        stacked,
        vmem(slab, f32),
        vmem((2 * N3, 2 * N3), bf16),
        vmem((2 * N3, 2 * N3), bf16),
        vmem((N3, 2 * N3), bf16),
        vmem((2 * N3, 2 * N3), bf16),
        vmem((2 * N3, 2 * N3), bf16),
        vmem((2 * N3, N3), bf16),
        vmem(slab, f32),
        vmem(slab, f32),
        vmem(slab, f32),
        vmem((N1, N3), f32),
        square,
        dma((10,)),
        dma((2,)),
    ] + [dma((GROUPS,))] * 12
    return pl.pallas_call(
        kernel,
        out_shape=(
            jax.ShapeDtypeStruct((1,) + slab, f32),
            jax.ShapeDtypeStruct((1,) + slab, f32),
        ),
        in_specs=[anywhere] * 6
        + [here, pl.BlockSpec(memory_space=pltpu.SMEM), here]
        + [anywhere] * 4,
        out_specs=(anywhere, anywhere),
        scratch_shapes=scratch,
        compiler_params=pltpu.CompilerParams(
            collective_id=0, has_side_effects=True, vmem_limit_bytes=66_000_000
        ),
        name="filter_step",
    )(
        states,
        potential,
        rotation_factor,
        basis_first,
        basis_second,
        basis_third,
        levels_first.reshape(N1 // N3, N3),
        levels_second,
        levels_third.reshape(1, N3),
        kinetic_first,
        kinetic_second,
        kinetic_third,
        coriolis_matrix,
    )


def solution(mesh):
    return jax.shard_map(
        per_device,
        mesh=mesh,
        in_specs=(
            P("ka", "coord", None, None),
            P("coord", None, None),
            P("coord", None),
            P(),
            P(),
            P(),
            P(),
            P(),
            P(),
            P(),
            P(),
            P(),
            P(),
        ),
        out_specs=(P("ka", "coord", None, None), P("ka", "coord", None, None)),
        check_vma=False,
    )
```

profile of v0, /device:TPU:1, one launch (start us, length us, event | category | flops | bytes accessed | tf_op | source)
XLA Modules:
  0.0 159.1 jit_solution(15901104706048266362)
XLA Ops:
  0.6 153.9 %filter_step.1 = (f32[1,8,512,128]{3,2,1,0:T(8,128)}, f32[1,8,512,128]{3,2,1,0:T(8,128)}) custom-call(f32[1,8,512,128]{3,2,1,0:T(8,128)} %states.1, f32[8,512,128]{2,1,0:T(8,128)} %potential.1, f32[8,512]{1,0:T(8,128)} %rotation.1, f32[512,512]{1,0:T(8,128)} %first.1, f32[512,512]{1,0:T(8,128)} %second.1, f32[128,128]{1,0:T(8,128)} %third.1, ...), custom_call_target="tpu_custom_call" | custom-call | tf_op jit(solution)/shard_map/filter_step/pallas_call | solution.py:706
  154.6 0.0 copy-start
  154.6 3.2 %copy.17 = f32[1,8,512,128]{3,2,1,0:T(8,128)} copy(f32[1,8,512,128]{3,2,1,0:T(8,128)} %get-tuple-element.4) | data formatting | bytes 4194304
  157.8 0.0 copy-done
  157.8 1.3 copy.18
Async XLA Ops:
  154.6 3.2 %copy-start = (f32[1,8,512,128]{3,2,1,0:T(8,128)S(1)}, f32[1,8,512,128]{3,2,1,0:T(8,128)}, u32[]{:S(2)}) copy-start(f32[1,8,512,128]{3,2,1,0:T(8,128)} %get-tuple-element.5) | copy-start | bytes 6291460
where the time goes:
time: 160 us; the launch traced here: 159 us
  Pallas kernels  154 us (96%)
  local copies, waits for them, and re-layouts  4.53 us (3%)
    pallas_call x1, Pallas kernels, per_device(): pl.pallas_call(kernel, out_shape=(jax.ShapeDtypeStruct((1,) + slab, f32),...  154 us
    unnamed x4, local copies, waits for them, and re-layouts  4.53 us

commit v1 on v0

--- a/solution.py
+++ b/solution.py
@@ -203,13 +203,20 @@
         for t in range(2):
             put_data(u1.at[pair], src[2 * pair + t], t * N3)
 
+    def strided(g, i):
+        return pl.ds(g * SPAN * ROWS + i, SPAN, stride=ROWS)
+
+    flat = (N2 * ROWS, N3)
+    u2_flat, xr_flat, yr_flat = u2.reshape(flat), xr.reshape(flat), yr.reshape(flat)
+    above_flat, below_flat = above.reshape(flat), below.reshape(flat)
+
     def way_out(g):
         rows = pl.ds(pl.multiple_of(g * SPAN, SPAN), SPAN)
         put_weight(w_b2t, b2[:, rows].T)
         for pair in range(PAIRS):
             out = dot(w_b2t[...], u1[pair])
-            u2[rows, 2 * pair, :] = out[:, 0:N3]
-            u2[rows, 2 * pair + 1, :] = out[:, N3:]
+            u2_flat[strided(g, 2 * pair), :] = out[:, 0:N3]
+            u2_flat[strided(g, 2 * pair + 1), :] = out[:, N3:]
 
         @pl.when(g == 0)
         def _():
@@ -345,7 +352,7 @@
             give_bent(g)
 
         for i in range(ROWS):
-            high, low = split(xr[rows, i, :])
+            high, low = split(xr_flat[strided(g, i), :])
             lx[i * SPAN : (i + 1) * SPAN, 0:N3] = high
             lx[i * SPAN : (i + 1) * SPAN, N3:] = low
 
@@ -383,10 +390,10 @@
 
         for i in range(ROWS):
             at = slice(i * SPAN, (i + 1) * SPAN)
-            high, low = split(above[rows, i, :])
+            high, low = split(above_flat[strided(g, i), :])
             lx[at, 0:N3] = high
             ly[at, 0:N3] = low
-            high, low = split(below[rows, i, :])
+            high, low = split(below_flat[strided(g, i), :])
             lx[at, N3:] = high
             ly[at, N3:] = low
 
@@ -589,7 +596,7 @@
         rows = pl.ds(pl.multiple_of(g * SPAN, SPAN), SPAN)
         pltpu.make_async_copy(yr.at[rows], yr.at[rows], y_recv.at[g]).wait()
         for i in range(ROWS):
-            high, low = split(yr[rows, i, :])
+            high, low = split(yr_flat[strided(g, i), :])
             ly[i * SPAN : (i + 1) * SPAN, 0:N3] = high
             ly[i * SPAN : (i + 1) * SPAN, N3:] = low
 
@@ -627,6 +634,28 @@
 
     for copy in results:
         copy.wait()
+
+
+def hand_out(solved, residual, solved_out, residual_out, held, in_sem, out_sem):
+    pieces = 4
+    ways = ((solved, solved_out), (residual, residual_out))
+    rows = [pl.ds(n * ROWS // pieces, ROWS // pieces) for n in range(pieces)]
+
+    def copies(way, n, inward):
+        source, target = ways[way]
+        here = held.at[way, rows[n]]
+        if inward:
+            return pltpu.make_async_copy(source.at[0, rows[n]], here, in_sem.at[way, n])
+        return pltpu.make_async_copy(here, target.at[0, rows[n]], out_sem.at[way, n])
+
+    order = [(way, n) for way in range(2) for n in range(pieces)]
+    for way, n in order:
+        copies(way, n, True).start()
+    for way, n in order:
+        copies(way, n, True).wait()
+        copies(way, n, False).start()
+    for way, n in order:
+        copies(way, n, False).wait()
 
 
 def per_device(
@@ -703,12 +732,10 @@
         dma((10,)),
         dma((2,)),
     ] + [dma((GROUPS,))] * 12
-    return pl.pallas_call(
+    shapes = (jax.ShapeDtypeStruct((1,) + slab, f32),) * 2
+    solved, residual = pl.pallas_call(
         kernel,
-        out_shape=(
-            jax.ShapeDtypeStruct((1,) + slab, f32),
-            jax.ShapeDtypeStruct((1,) + slab, f32),
-        ),
+        out_shape=shapes,
         in_specs=[anywhere] * 6
         + [here, pl.BlockSpec(memory_space=pltpu.SMEM), here]
         + [anywhere] * 4,
@@ -733,6 +760,14 @@
         kinetic_third,
         coriolis_matrix,
     )
+    return pl.pallas_call(
+        hand_out,
+        out_shape=shapes,
+        in_specs=[anywhere] * 2,
+        out_specs=(anywhere,) * 2,
+        scratch_shapes=[vmem((2,) + slab, f32), dma((2, 4)), dma((2, 4))],
+        name="tail",
+    )(solved, residual)
 
 
 def solution(mesh):

time: 160 us -> 155 us (0.969)
  local copies, waits for them, and re-layouts: 4.53 us -> 0 us
    unnamed x4 -> x0, local copies, waits for them, and re-layouts: 4.53 us -> none
    pallas_call x1 -> x2, Pallas kernels: 154 us -> 153 us  [the longest x1 149 us: per_device(): pl.pallas_call(kernel, out_shape=shapes, in_specs=[anywhere] * 6 + [here,...]
where the time goes in v1:
time: 155 us; the launch traced here: 154 us
  Pallas kernels  153 us (99%)
    pallas_call x1, Pallas kernels, per_device(): pl.pallas_call(kernel, out_shape=shapes, in_specs=[anywhere] * 6 + [here,...  149 us
    pallas_call x1, Pallas kernels, per_device(): pl.pallas_call(hand_out, out_shape=shapes, in_specs=[anywhere] * 2, out_s...  3.58 us

profile of v1, /device:TPU:1, one launch (start us, length us, event | category | flops | bytes accessed | tf_op | source)
XLA Modules:
  0.0 153.5 jit_solution(39366871726381574)
XLA Ops:
  0.6 149.3 %filter_step.1 = (f32[1,8,512,128]{3,2,1,0:T(8,128)}, f32[1,8,512,128]{3,2,1,0:T(8,128)}) custom-call(f32[1,8,512,128]{3,2,1,0:T(8,128)} %states.1, f32[8,512,128]{2,1,0:T(8,128)} %potential.1, f32[8,512]{1,0:T(8,128)} %rotation.1, f32[512,512]{1,0:T(8,128)} %first.1, f32[512,512]{1,0:T(8,128)} %second.1, f32[128,128]{1,0:T(8,128)} %third.1, ...), custom_call_target="tpu_custom_call" | custom-call | tf_op jit(solution)/shard_map/filter_step/pallas_call | solution.py:736
  149.9 3.6 %tail.1 = (f32[1,8,512,128]{3,2,1,0:T(8,128)}, f32[1,8,512,128]{3,2,1,0:T(8,128)}) custom-call(f32[1,8,512,128]{3,2,1,0:T(8,128)} %get-tuple-element.4.solved, f32[1,8,512,128]{3,2,1,0:T(8,128)} %get-tuple-element.5.residual), custom_call_target="tpu_custom_call" | custom-call | tf_op jit(solution)/shard_map/tail/pallas_call | solution.py:763

commit v2 on v1

--- a/solution.py
+++ b/solution.py
@@ -343,13 +343,7 @@
                 device_id_type=MESH,
             ).start()
 
-        @pl.when(g > 0)
-        def _():
-            give_bent(g - 1)
-
-        @pl.when(g == GROUPS - 1)
-        def _():
-            give_bent(g)
+        give_bent(g)
 
         for i in range(ROWS):
             high, low = split(xr_flat[strided(g, i), :])
@@ -377,7 +371,7 @@
                 for t in range(2):
                     src[2 * pair + t] -= out[:, t * N3 : (t + 1) * N3]
 
-    def between_blocks(g, last=False):
+    def between_blocks(g):
         rows = pl.ds(pl.multiple_of(g * SPAN, SPAN), SPAN)
 
         @pl.when(ka < BLOCKS - 1)
@@ -414,12 +408,6 @@
                 out = dot(w_b2[:, both], tv[pair])
                 for t in range(2):
                     acc_v[2 * pair + t] += out[:, t * N3 : (t + 1) * N3]
-                if last:
-                    two = pl.ds(2 * pair, 2)
-                    src[two] -= wide[two] * acc_v[two]
-                    pltpu.make_async_copy(
-                        src.at[two], residual_out.at[0, two], out_sem.at[1]
-                    ).start()
 
     way_out(0)
 
@@ -591,8 +579,7 @@
     def _(i):
         src[i] -= diag[i] * pot[i]
 
-    @pl.loop(0, GROUPS)
-    def _(g):
+    def bent_in_slab(g, last=False):
         rows = pl.ds(pl.multiple_of(g * SPAN, SPAN), SPAN)
         pltpu.make_async_copy(yr.at[rows], yr.at[rows], y_recv.at[g]).wait()
         for i in range(ROWS):
@@ -611,8 +598,16 @@
             out = dot(w_b2[:, each], t2[pair])
             for t in range(2):
                 src[2 * pair + t] -= out[:, t * N3 : (t + 1) * N3]
-
-    between_blocks(GROUPS - 1, last=True)
+            if last:
+                two = pl.ds(2 * pair, 2)
+                src[two] -= wide[two] * acc_v[two]
+                pltpu.make_async_copy(
+                    src.at[two], residual_out.at[0, two], out_sem.at[1]
+                ).start()
+
+    pl.loop(0, GROUPS - 1)(bent_in_slab)
+    between_blocks(GROUPS - 1)
+    bent_in_slab(GROUPS - 1, last=True)
     results.append(pltpu.make_async_copy(src, residual_out.at[0], out_sem.at[1]))
 
     @pl.loop(0, GROUPS)
@@ -637,7 +632,7 @@
 
 
 def hand_out(solved, residual, solved_out, residual_out, held, in_sem, out_sem):
-    pieces = 4
+    pieces = 8
     ways = ((solved, solved_out), (residual, residual_out))
     rows = [pl.ds(n * ROWS // pieces, ROWS // pieces) for n in range(pieces)]
 
@@ -765,7 +760,7 @@
         out_shape=shapes,
         in_specs=[anywhere] * 2,
         out_specs=(anywhere,) * 2,
-        scratch_shapes=[vmem((2,) + slab, f32), dma((2, 4)), dma((2, 4))],
+        scratch_shapes=[vmem((2,) + slab, f32), dma((2, 8)), dma((2, 8))],
         name="tail",
     )(solved, residual)
 

time: 155 us -> 154 us (level)
  no operation moved by 1% of the time
where the time goes in v2:
time: 154 us
  Pallas kernels  153 us (99%)
    pallas_call x1, Pallas kernels, per_device(): pl.pallas_call(kernel, out_shape=shapes, in_specs=[anywhere] * 6 + [here,...  150 us
    pallas_call x1, Pallas kernels, per_device(): pl.pallas_call(hand_out, out_shape=shapes, in_specs=[anywhere] * 2, out_s...  3.85 us

profile of v2, /device:TPU:1, one launch (start us, length us, event | category | flops | bytes accessed | tf_op | source)
XLA Modules:
  0.0 154.0 jit_solution(1372458547544718953)
XLA Ops:
  0.6 149.5 %filter_step.1 = (f32[1,8,512,128]{3,2,1,0:T(8,128)}, f32[1,8,512,128]{3,2,1,0:T(8,128)}) custom-call(f32[1,8,512,128]{3,2,1,0:T(8,128)} %states.1, f32[8,512,128]{2,1,0:T(8,128)} %potential.1, f32[8,512]{1,0:T(8,128)} %rotation.1, f32[512,512]{1,0:T(8,128)} %first.1, f32[512,512]{1,0:T(8,128)} %second.1, f32[128,128]{1,0:T(8,128)} %third.1, ...), custom_call_target="tpu_custom_call" | custom-call | tf_op jit(solution)/shard_map/filter_step/pallas_call | solution.py:731
  150.1 3.9 %tail.1 = (f32[1,8,512,128]{3,2,1,0:T(8,128)}, f32[1,8,512,128]{3,2,1,0:T(8,128)}) custom-call(f32[1,8,512,128]{3,2,1,0:T(8,128)} %get-tuple-element.4.solved, f32[1,8,512,128]{3,2,1,0:T(8,128)} %get-tuple-element.5.residual), custom_call_target="tpu_custom_call" | custom-call | tf_op jit(solution)/shard_map/tail/pallas_call | solution.py:758
